TPU v7x, 32 devices: a whole 2x2x4 slice. The times are simulated.
32 devices in a mesh: section: 4 (over z), tile: 8 (over y, x, core).
Axes of the slice: x: 2, y: 2, z: 4, core: 2. Of those that a mesh axis runs over, the one named last changes fastest.
Arguments:
- raw_echo: bfloat16 [2, 2048, 8192], P(None, 'tile', 'section'), may hold values from -6 to 6
- footprint: int32 [4, 8, 8], P('section', 'tile'), may hold values from 0 to 255, as said below
- window_start: int32 [4, 256], P('section', 'tile'), may hold values from 0 to 2047
Outputs:
- image: bfloat16 [4, 8, 1024, 2048], P('section', 'tile')
Inputs may be any that keep to these rules, and one draw needn't show every extreme that they name: `footprint`: each list names 8 different pulse blocks; at most 2 of them lie among the 32 blocks k * 32 to (k + 1) * 32 - 1 of one index k of tile, and in every list some index supplies exactly 2.
All inputs are finite; a program needn't handle non-finite values.
Results may differ from a plain program's by a relative error of at most 0.0071.
Values may be sent and summed in bfloat16 or wider, within the bound.
No kernel may reach another device: no remote copies, remote signals or barrier semaphores. Data moves between devices by JAX's collectives and lax.ppermute only.
A program may use at most 128 MiB of HBM per device.

v0:
```python
import math
import jax
import jax.numpy as jnp
from jax import lax
from jax.sharding import PartitionSpec as P

KC = 128
WIN = 256
PR = 1024
PC = 1024
NP = 8


def passed_along(value, axis, by):
    devices = lax.axis_size(axis)
    pairs = [(i, i + by) for i in range(devices) if 0 <= i + by < devices]
    return lax.ppermute(value, axis, pairs)


def chirp_table(length):
    row_index = lax.broadcasted_iota(jnp.int32, (2 * length, length), 0)
    col_index = lax.broadcasted_iota(jnp.int32, (2 * length, length), 1)
    lag_count = row_index - col_index
    inside = (lag_count >= 0) & (lag_count < length)
    lag_safe = jnp.where(inside, lag_count, 0)
    turn_count = (lag_safe * lag_safe % (2 * length)).astype(jnp.float32)
    phase_angle = turn_count * jnp.float32(math.pi / length)
    scaling = jnp.float32(1.0 / math.sqrt(length))
    real_part = jnp.where(inside, jnp.cos(phase_angle) * scaling, jnp.float32(0.0))
    imag_part = jnp.where(inside, jnp.sin(phase_angle) * scaling, jnp.float32(0.0))
    return (real_part.astype(jnp.bfloat16), imag_part.astype(jnp.bfloat16))


def compress(raw_part, length, keep):
    real_tab, imag_tab = chirp_table(length)
    pulses = raw_part.shape[1]
    blocks = keep // length
    pieces = raw_part.reshape(2, pulses, blocks + 1, length)
    paired = jnp.concatenate([pieces[:, :, :-1], pieces[:, :, 1:]], axis=3).reshape(
        2, pulses * blocks, 2 * length
    )
    real_in = paired[0]
    imag_in = paired[1]
    out_real = jnp.dot(real_in, real_tab, preferred_element_type=jnp.float32) + jnp.dot(
        imag_in, imag_tab, preferred_element_type=jnp.float32
    )
    out_imag = jnp.dot(imag_in, real_tab, preferred_element_type=jnp.float32) - jnp.dot(
        real_in, imag_tab, preferred_element_type=jnp.float32
    )
    stacked = jnp.stack([out_real, out_imag]).reshape(2, pulses, keep)
    return stacked.astype(jnp.bfloat16)


def interp_table(pixel_rows, window_bins):
    upsample = pixel_rows // window_bins
    row_index = lax.broadcasted_iota(jnp.float32, (pixel_rows, window_bins), 0)
    bin_index = lax.broadcasted_iota(jnp.float32, (pixel_rows, window_bins), 1)
    centre = (row_index + 0.5) / upsample - 0.5
    offset = bin_index - centre
    tapering = jnp.cos(offset * (math.pi / 8.0)) ** 2
    kernel = jnp.where(jnp.abs(offset) < 4.0, jnp.sinc(offset) * tapering, 0.0)
    return kernel.astype(jnp.bfloat16)


def tile_image(chosen, block_ids, row_pos, col_pos, interp, pixel_cols):
    entries = chosen.shape[0]
    per_block = chosen.shape[1]
    window_bins = chosen.shape[3]
    merged = chosen.reshape(entries * per_block, 2 * window_bins)
    pulse_ids = (
        block_ids[:, None] * per_block + jnp.arange(per_block, dtype=jnp.int32)[None, :]
    ).reshape(-1)
    columns = col_pos * pixel_cols + jnp.arange(pixel_cols, dtype=jnp.int32) + 1 + 7 * row_pos
    scrambled = columns * 40503 % 65521
    residue = pulse_ids[:, None] * scrambled[None, :] % 65521
    phase_angle = residue.astype(jnp.float32) * jnp.float32(2.0 * math.pi / 65521.0)
    steer_real = jnp.cos(phase_angle).astype(jnp.bfloat16)
    steer_imag = jnp.sin(phase_angle).astype(jnp.bfloat16)
    contract = (((0,), (0,)), ((), ()))
    with_real = lax.dot_general(merged, steer_real, contract, preferred_element_type=jnp.float32)
    with_imag = lax.dot_general(merged, steer_imag, contract, preferred_element_type=jnp.float32)
    scaling = jnp.float32(1.0 / math.sqrt(entries * per_block))
    focus_real = (with_real[:window_bins] - with_imag[window_bins:]) * scaling
    focus_imag = (with_imag[:window_bins] + with_real[window_bins:]) * scaling
    focused = jnp.concatenate([focus_real, focus_imag], axis=1).astype(jnp.bfloat16)
    return jnp.dot(interp, focused, preferred_element_type=jnp.float32).astype(jnp.bfloat16)


def cut_windows(extended, starts, per_block):
    pulses = extended.shape[1]
    span_bins = extended.shape[2]
    grouped = jnp.transpose(
        extended.reshape(2, pulses // per_block, per_block, span_bins), (1, 2, 0, 3)
    )

    def one_block(block_data, start):
        return lax.dynamic_slice_in_dim(block_data, start, WIN, 2)

    return jax.vmap(one_block)(grouped, starts)


def local(raw_echo, footprint, window_start):
    bin_count = raw_echo.shape[2]
    next_rim = passed_along(raw_echo[:, :, :KC], "section", -1)
    own_part = compress(jnp.concatenate([raw_echo, next_rim], axis=2), KC, bin_count)
    next_bins = passed_along(own_part[:, :, :WIN], "section", -1)
    extended = jnp.concatenate([own_part, next_bins], axis=2)
    windows = cut_windows(extended, window_start[0], NP)
    my_list = footprint[0, 0]
    tile_pos = lax.axis_index("tile")
    row_pos = lax.axis_index("section")
    all_blocks = lax.all_gather(windows, "tile", axis=0, tiled=True)
    chosen = jnp.take(all_blocks, my_list, axis=0)
    interp = interp_table(PR, WIN)
    image = tile_image(chosen, my_list, row_pos, tile_pos, interp, PC)
    return image[None, None]


def solution(mesh):
    in_specs = (P(None, "tile", "section"), P("section", "tile", None), P("section", "tile"))
    out_specs = P("section", "tile", None, None)
    return jax.shard_map(local, mesh=mesh, in_specs=in_specs, out_specs=out_specs, check_vma=False)
```

profile of v0, /device:TPU:0, one launch (start us, length us, event | category | flops | bytes accessed | tf_op | source)
XLA Modules:
  0.0 181.1 jit_solution(12100500757804425028)
XLA Ops:
  6.5 2.8 %copy.15 = bf16[2,256,2048]{1,2,0:T(8,128)(2,1)S(1)} copy(bf16[2,256,2048]{2,1,0:T(8,128)(2,1)} %param.3) | data formatting | bytes 4194304 | tf_op args[0]
  9.4 1.3 collective-permute-start
  10.7 7.1 %collective-permute-done = bf16[2,256,128]{1,2,0:T(8,128)(2,1)S(1)} collective-permute-done((bf16[2,256,128]{1,2,0:T(8,128)(2,1)S(1)}, bf16[2,256,128]{1,2,0:T(8,128)(2,1)S(1)}, u32[]{:S(2)}, u32[]{:S(2)}) %collective-permute-start) | collective-permute-done | bytes 131104 | tf_op jit(solution)/shard_map/ppermute | solution.py:17
  18.0 0.5 fusion.123
  18.5 2.3 %pad_maximum_fusion.1 = (bf16[1,256,16,256]{1,3,2,0:T(8,128)(2,1)}, bf16[1,256,16,256]{1,3,2,0:T(8,128)(2,1)}) fusion(bf16[2,256,16,128]{1,3,2,0:T(8,128)(2,1)S(1)} %get-tuple-element.9, bf16[2,256,16,128]{1,3,2,0:T(8,128)(2,1)S(1)} %get-tuple-element.10), kind=kLoop, calls=%fused_computation.12 | loop fusion | flops 8388608 | bytes 8388608 | tf_op jit(solution)/shard_map/concatenate | solution.py:39
  20.8 3.3 %copy.17 = bf16[1,256,16,256]{3,2,1,0:T(8,128)(2,1)S(1)} copy(bf16[1,256,16,256]{1,3,2,0:T(8,128)(2,1)} %get-tuple-element.7) | data formatting | bytes 4194304 | tf_op jit(solution)/shard_map/slice | solution.py:43
  24.1 2.5 %fusion.63 = f32[4096,128]{1,0:T(8,128)} fusion(bf16[4096,256]{1,0:T(8,128)(2,1)S(1)} %bitcast.27), kind=kOutput, calls=%fused_computation.95 | convolution fusion | flops 269156352 | bytes 4194304 | tf_op jit(solution)/shard_map/dot_general | solution.py:47
  26.6 4.5 %copy.16 = bf16[1,256,16,256]{3,2,1,0:T(8,128)(2,1)} copy(bf16[1,256,16,256]{1,3,2,0:T(8,128)(2,1)} %get-tuple-element.8) | data formatting | bytes 4194304 | tf_op jit(solution)/shard_map/slice | solution.py:42
  31.1 4.2 %fusion.64 = f32[4096,128]{1,0:T(8,128)} fusion(bf16[4096,256]{1,0:T(8,128)(2,1)} %bitcast.29), kind=kOutput, calls=%fused_computation.96 | convolution fusion | flops 269156352 | bytes 4194304 | tf_op jit(solution)/shard_map/dot_general | solution.py:44
  35.4 1.2 fusion.1
  36.6 1.3 stack.10
  37.9 2.8 %fusion = bf16[4096,128]{1,0:T(8,128)(2,1)S(1)} fusion(f32[4096,128]{1,0:T(8,128)} %fusion.64, bf16[4096,256]{1,0:T(8,128)(2,1)S(1)} %bitcast.28), kind=kOutput, calls=%fused_computation.4 | convolution fusion | flops 270204928 | bytes 5242880 | tf_op jit(solution)/shard_map/dot_general | solution.py:44
  41.3 0.6 copy-done.2
  42.0 1.5 collective-permute-start.1
  43.5 7.9 %collective-permute-done.1 = bf16[2,256,256]{2,1,0:T(8,128)(2,1)S(1)} collective-permute-done((bf16[2,256,256]{2,1,0:T(8,128)(2,1)S(1)}, bf16[2,256,256]{2,1,0:T(8,128)(2,1)S(1)}, u32[]{:S(2)}, u32[]{:S(2)}) %collective-permute-start.1) | collective-permute-done | bytes 262176 | tf_op jit(solution)/shard_map/ppermute | solution.py:17
  51.6 60.6 %copy.18 = bf16[2,32,8,2304]{2,0,1,3:T(2,128)(2,1)} copy(bf16[2,32,8,2304]{3,2,1,0:T(8,128)(2,1)S(1)} %maximum_bitcast_fusion) | data formatting | bytes 4718592 | tf_op jit(solution)/shard_map/reshape | solution.py:93
  112.2 11.5 %gather_fusion.1 = bf16[32,8,2,256]{1,2,3,0:T(2,128)(2,1)} fusion(bf16[32,8,2,2304]{1,2,0,3:T(2,128)(2,1)} %bitcast.26, s32[32]{0:T(128)S(1)} %fusion.72), kind=kCustom, calls=%fused_computation.1 | custom fusion | bytes 524800 | tf_op jit(solution)/shard_map/vmap()/gather | solution.py:97
  123.8 9.2 %copy.19 = bf16[32,8,2,256]{3,1,2,0:T(8,128)(2,1)} copy(bf16[32,8,2,256]{1,2,3,0:T(2,128)(2,1)} %gather_fusion.1) | data formatting | bytes 524288 | tf_op jit(solution)/shard_map/vmap()/gather | solution.py:97
  133.4 27.7 %all-gather.2.cloned.1.call-done = bf16[256,8,2,256]{3,1,2,0:T(8,128)(2,1)} async-done(((bf16[32,8,2,256]{3,1,2,0:T(8,128)(2,1)}), bf16[256,8,2,256]{3,1,2,0:T(8,128)(2,1)}) %all-gather.2.cloned.1.call-update) | async-done | bytes 2097168 | tf_op jit(solution)/shard_map/all_gather | solution.py:112
  161.1 2.1 %gather_fusion = bf16[8,8,2,256]{3,1,2,0:T(8,128)(2,1)S(1)} fusion(bf16[256,8,2,256]{3,1,2,0:T(8,128)(2,1)} %all-gather.2.cloned.1.call-done, s32[1024]{0:T(1024)S(1)} %pad_clamp_fusion), kind=kCustom, calls=%fused_computation | custom fusion | bytes 131104 | tf_op jit(solution)/shard_map/jit(_take)/gather | solution.py:113
  163.3 1.4 fusion.48
  164.7 1.4 fusion.49
  166.1 0.5 fusion.14
  166.6 7.6 %convert_bitcast_fusion = bf16[1,1,1024,2048]{3,2,1,0:T(8,128)(2,1)} fusion(bf16[256,1024]{1,0:T(8,128)(2,1)S(1)} %get-tuple-element.6, bf16[256,1024]{1,0:T(8,128)(2,1)S(1)} %get-tuple-element.5, f32[1024]{0:T(1024)S(1)} %multiply_add_fusion.1), kind=kOutput, calls=%fused_computation.8 | convolution fusion | flops 1088421888 | bytes 5246976 | tf_op jit(solution)/shard_map/dot_general | solution.py:86
  (29 shorter events, 1.4 us)
Async XLA Ops:
  6.5 154.6 %all-gather.2.cloned.1.call-start = ((), (), s32[]{:S(2)}) async-start(), calls=%async_computation | async-start | bytes 2359296 | tf_op jit(solution)/shard_map/all_gather | solution.py:112
  9.4 8.4 %collective-permute-start = (bf16[2,256,128]{1,2,0:T(8,128)(2,1)S(1)}, bf16[2,256,128]{1,2,0:T(8,128)(2,1)S(1)}, u32[]{:S(2)}, u32[]{:S(2)}) collective-permute-start(bf16[2,256,128]{1,2,0:T(8,128)(2,1)S(1)} %slice.51), channel_id=1, source_target_pairs={{8,0},{16,8},{24,16},{9,1},{17,9},{25,17},{10,2},{18,10},{26,18},{... | collective-permute-start | bytes 393224 | tf_op jit(solution)/shard_map/ppermute | solution.py:17
  31.1 4.3 %copy-start = (bf16[1,256,16,256]{3,2,1,0:T(8,128)(2,1)S(1)}, bf16[1,256,16,256]{3,2,1,0:T(8,128)(2,1)}, u32[]{:S(2)}) copy-start(bf16[1,256,16,256]{3,2,1,0:T(8,128)(2,1)} %copy.16) | copy-start | bytes 6291460
  31.1 4.3 %copy-start.1 = (f32[4096,128]{1,0:T(8,128)S(1)}, f32[4096,128]{1,0:T(8,128)}, u32[]{:S(2)}) copy-start(f32[4096,128]{1,0:T(8,128)} %fusion.63) | copy-start | bytes 6291460
  40.7 1.2 copy-start.2
  41.2 2.3 %copy-start.3 = (s32[1,32]{1,0:T(1,128)S(1)}, s32[1,32]{1,0:T(1,128)}, u32[]{:S(2)}) copy-start(s32[1,32]{1,0:T(1,128)} %param.5) | copy-start | bytes 388
  42.0 9.4 %collective-permute-start.1 = (bf16[2,256,256]{2,1,0:T(8,128)(2,1)S(1)}, bf16[2,256,256]{2,1,0:T(8,128)(2,1)S(1)}, u32[]{:S(2)}, u32[]{:S(2)}) collective-permute-start(bf16[2,256,256]{2,1,0:T(8,128)(2,1)S(1)} %slice.56), channel_id=1, source_target_pairs={{8,0},{16,8},{24,16},{9,1},{17,9},{25,17},{10,2},{18,10},{26,18},{... | collective-permute-start | bytes 786440 | tf_op jit(solution)/shard_map/ppermute | solution.py:17
  123.8 9.2 %copy-start.4 = (s32[1,1,8]{2,1,0:T(1,128)S(1)}, s32[1,1,8]{2,1,0:T(1,128)}, u32[]{:S(2)}) copy-start(s32[1,1,8]{2,1,0:T(1,128)} %param.4) | copy-start | bytes 100
Sparse Core Ops, SparseCore 0:
  133.1 27.9 all-gather.1
where the time goes:
time: 182 us; the launch traced here: 181 us
  local copies, waits for them, and re-layouts  97.6 us (54%)
  waiting for transfers between devices  42.7 us (23%)
  matrix products  21.3 us (12%)
  between operations  13.6 us (7%)
  other arithmetic  3.22 us (2%)
  starting transfers between devices  2.77 us (2%)
    reshape x1, local copies, waits for them, and re-layouts, cut_windows(): extended.reshape(2, pulses // per_block, per_block, span_bins)  60.6 us
    all_gather x1, waiting for transfers between devices, local(): all_blocks = lax.all_gather(windows, 'tile', axis=0, tiled=True)  27.7 us
    gather x2, local copies, waits for them, and re-layouts, one_block(): return lax.dynamic_slice_in_dim(block_data, start, WIN, 2)  20.7 us
    ppermute x2, waiting for transfers between devices, passed_along(): return lax.ppermute(value, axis, pairs)  15 us
    dot_general x1, matrix products, tile_image(): jnp.dot(interp, focused, preferred_element_type=jnp.float32)  7.65 us
    slice x1, local copies, waits for them, and re-layouts, compress(): real_in = paired[0]  4.49 us
    dot_general x1, matrix products, compress(): jnp.dot(real_in, real_tab, preferred_element_type=jnp.float32)  4.25 us
  transfers between devices with their start and end apart: 3, of which 3 were waited for; matrix products, arithmetic and copies ran while one was open for 0% of the time, Pallas kernels for 0%

commit v1 on v0

--- a/solution.py
+++ b/solution.py
@@ -109,7 +109,14 @@
     my_list = footprint[0, 0]
     tile_pos = lax.axis_index("tile")
     row_pos = lax.axis_index("section")
-    all_blocks = lax.all_gather(windows, "tile", axis=0, tiled=True)
+    x = windows
+    ways, here, step = (lax.axis_size("tile"), lax.axis_index("tile"), x.shape[0])
+    lengths = [n * ways if d == 0 else n for d, n in enumerate(x.shape)]
+    full = lax.dynamic_update_slice_in_dim(jnp.zeros(lengths, x.dtype), x, here * step, axis=0)
+    for far in range(1, ways):
+        x = lax.ppermute(x, "tile", [(d, (d + 1) % ways) for d in range(ways)])
+        full = lax.dynamic_update_slice_in_dim(full, x, (here - far) % ways * step, axis=0)
+    all_blocks = full
     chosen = jnp.take(all_blocks, my_list, axis=0)
     interp = interp_table(PR, WIN)
     image = tile_image(chosen, my_list, row_pos, tile_pos, interp, PC)

time: 182 us -> 185 us (1.016)
  waiting for transfers between devices: 42.7 us -> 60.5 us
  between operations: 13.6 us -> 0.4 us
    ppermute x0 -> x7, waiting for transfers between devices: none -> 45.3 us  [local(): x = lax.ppermute(x, 'tile', [(d, (d + 1) % ways) for d in range(ways)])]
    all_gather x1 -> x0, waiting for transfers between devices: 27.7 us -> none  [local(): all_blocks = lax.all_gather(windows, 'tile', axis=0, tiled=True)]
  transfers between devices with their start and end apart: 3 -> 9, of which waited for: 3 -> 9; matrix products, arithmetic and copies ran while one was open for 0% -> 1% of each run, Pallas kernels for 0% -> 0%
where the time goes in v1:
time: 185 us; the launch traced here: 184 us
  local copies, waits for them, and re-layouts  96.2 us (52%)
  waiting for transfers between devices  60.5 us (33%)
  matrix products  21.3 us (12%)
  other arithmetic  3.23 us (2%)
  starting transfers between devices  2.66 us (1%)
    reshape x1, local copies, waits for them, and re-layouts, cut_windows(): extended.reshape(2, pulses // per_block, per_block, span_bins)  60.7 us
    ppermute x7, waiting for transfers between devices, local(): x = lax.ppermute(x, 'tile', [(d, (d + 1) % ways) for d in range(ways)])  45.3 us
    gather x2, local copies, waits for them, and re-layouts, one_block(): return lax.dynamic_slice_in_dim(block_data, start, WIN, 2)  19.7 us
    ppermute x2, waiting for transfers between devices, passed_along(): return lax.ppermute(value, axis, pairs)  15.2 us
    dot_general x1, matrix products, tile_image(): jnp.dot(interp, focused, preferred_element_type=jnp.float32)  7.65 us
    slice x1, local copies, waits for them, and re-layouts, compress(): real_in = paired[0]  4.49 us
    dot_general x1, matrix products, compress(): jnp.dot(real_in, real_tab, preferred_element_type=jnp.float32)  4.27 us
  transfers between devices with their start and end apart: 9, of which 9 were waited for; matrix products, arithmetic and copies ran while one was open for 1% of the time, Pallas kernels for 0%

profile of v1, /device:TPU:0, one launch (start us, length us, event | category | flops | bytes accessed | tf_op | source)
XLA Modules:
  0.0 184.3 jit_solution(6999003186506012455)
XLA Ops:
  0.0 2.8 %copy.21 = bf16[2,256,2048]{1,2,0:T(8,128)(2,1)S(1)} copy(bf16[2,256,2048]{2,1,0:T(8,128)(2,1)} %param.3) | data formatting | bytes 4194304 | tf_op args[0]
  2.9 1.3 collective-permute-start
  4.2 7.1 %collective-permute-done = bf16[2,256,128]{1,2,0:T(8,128)(2,1)S(1)} collective-permute-done((bf16[2,256,128]{1,2,0:T(8,128)(2,1)S(1)}, bf16[2,256,128]{1,2,0:T(8,128)(2,1)S(1)}, u32[]{:S(2)}, u32[]{:S(2)}) %collective-permute-start) | collective-permute-done | bytes 131104 | tf_op jit(solution)/shard_map/ppermute | solution.py:17
  12.0 2.3 %pad_maximum_fusion.1 = (bf16[1,256,16,256]{1,3,2,0:T(8,128)(2,1)}, bf16[1,256,16,256]{1,3,2,0:T(8,128)(2,1)}) fusion(bf16[2,256,16,128]{1,3,2,0:T(8,128)(2,1)S(1)} %get-tuple-element.9, bf16[2,256,16,128]{1,3,2,0:T(8,128)(2,1)S(1)} %get-tuple-element.10), kind=kLoop, calls=%fused_computation.12 | loop fusion | flops 8388608 | bytes 8388608 | tf_op jit(solution)/shard_map/concatenate | solution.py:39
  14.2 3.3 %copy.23 = bf16[1,256,16,256]{3,2,1,0:T(8,128)(2,1)S(1)} copy(bf16[1,256,16,256]{1,3,2,0:T(8,128)(2,1)} %get-tuple-element.7) | data formatting | bytes 4194304 | tf_op jit(solution)/shard_map/slice | solution.py:43
  17.6 2.5 %fusion.63 = f32[4096,128]{1,0:T(8,128)} fusion(bf16[4096,256]{1,0:T(8,128)(2,1)S(1)} %bitcast.27), kind=kOutput, calls=%fused_computation.95 | convolution fusion | flops 269156352 | bytes 4194304 | tf_op jit(solution)/shard_map/dot_general | solution.py:47
  20.1 4.5 %copy.22 = bf16[1,256,16,256]{3,2,1,0:T(8,128)(2,1)} copy(bf16[1,256,16,256]{1,3,2,0:T(8,128)(2,1)} %get-tuple-element.8) | data formatting | bytes 4194304 | tf_op jit(solution)/shard_map/slice | solution.py:42
  24.6 4.3 %fusion.64 = f32[4096,128]{1,0:T(8,128)} fusion(bf16[4096,256]{1,0:T(8,128)(2,1)} %bitcast.29), kind=kOutput, calls=%fused_computation.96 | convolution fusion | flops 269156352 | bytes 4194304 | tf_op jit(solution)/shard_map/dot_general | solution.py:44
  31.4 2.8 %fusion = bf16[4096,128]{1,0:T(8,128)(2,1)S(1)} fusion(f32[4096,128]{1,0:T(8,128)} %fusion.64, bf16[4096,256]{1,0:T(8,128)(2,1)S(1)} %bitcast.28), kind=kOutput, calls=%fused_computation.4 | convolution fusion | flops 270204928 | bytes 5242880 | tf_op jit(solution)/shard_map/dot_general | solution.py:44
  35.5 1.3 collective-permute-start.1
  36.8 8.1 %collective-permute-done.1 = bf16[2,256,256]{2,1,0:T(8,128)(2,1)S(1)} collective-permute-done((bf16[2,256,256]{2,1,0:T(8,128)(2,1)S(1)}, bf16[2,256,256]{2,1,0:T(8,128)(2,1)S(1)}, u32[]{:S(2)}, u32[]{:S(2)}) %collective-permute-start.1) | collective-permute-done | bytes 262176 | tf_op jit(solution)/shard_map/ppermute | solution.py:17
  45.1 60.7 %copy.24 = bf16[2,32,8,2304]{2,0,1,3:T(2,128)(2,1)} copy(bf16[2,32,8,2304]{3,2,1,0:T(8,128)(2,1)S(1)} %maximum_bitcast_fusion) | data formatting | bytes 4718592 | tf_op jit(solution)/shard_map/reshape | solution.py:93
  105.8 11.5 %gather_fusion.1 = bf16[32,8,2,256]{1,2,3,0:T(2,128)(2,1)} fusion(bf16[32,8,2,2304]{1,2,0,3:T(2,128)(2,1)} %bitcast.26, s32[32]{0:T(128)S(1)} %fusion.78), kind=kCustom, calls=%fused_computation.1 | custom fusion | bytes 524800 | tf_op jit(solution)/shard_map/vmap()/gather | solution.py:97
  117.3 8.1 %copy.25 = bf16[32,8,2,256]{3,1,2,0:T(8,128)(2,1)S(1)} copy(bf16[32,8,2,256]{1,2,3,0:T(2,128)(2,1)} %gather_fusion.1) | data formatting | bytes 524288 | tf_op jit(solution)/shard_map/vmap()/gather | solution.py:97
  125.6 6.7 %collective-permute-done.2 = bf16[32,8,2,256]{3,1,2,0:T(8,128)(2,1)S(1)} collective-permute-done((bf16[32,8,2,256]{3,1,2,0:T(8,128)(2,1)S(1)}, bf16[32,8,2,256]{3,1,2,0:T(8,128)(2,1)S(1)}, u32[]{:S(2)}, u32[]{:S(2)}) %collective-permute-start.2) | collective-permute-done | bytes 262176 | tf_op jit(solution)/shard_map/ppermute | solution.py:117
  132.2 6.7 %collective-permute-done.3 = bf16[32,8,2,256]{3,1,2,0:T(8,128)(2,1)S(1)} collective-permute-done((bf16[32,8,2,256]{3,1,2,0:T(8,128)(2,1)S(1)}, bf16[32,8,2,256]{3,1,2,0:T(8,128)(2,1)S(1)}, u32[]{:S(2)}, u32[]{:S(2)}) %collective-permute-start.3) | collective-permute-done | bytes 262176 | tf_op jit(solution)/shard_map/ppermute | solution.py:117
  138.9 6.7 %collective-permute-done.4 = bf16[32,8,2,256]{3,1,2,0:T(8,128)(2,1)S(1)} collective-permute-done((bf16[32,8,2,256]{3,1,2,0:T(8,128)(2,1)S(1)}, bf16[32,8,2,256]{3,1,2,0:T(8,128)(2,1)S(1)}, u32[]{:S(2)}, u32[]{:S(2)}) %collective-permute-start.4) | collective-permute-done | bytes 262176 | tf_op jit(solution)/shard_map/ppermute | solution.py:117
  145.7 6.6 %collective-permute-done.5 = bf16[32,8,2,256]{3,1,2,0:T(8,128)(2,1)S(1)} collective-permute-done((bf16[32,8,2,256]{3,1,2,0:T(8,128)(2,1)S(1)}, bf16[32,8,2,256]{3,1,2,0:T(8,128)(2,1)S(1)}, u32[]{:S(2)}, u32[]{:S(2)}) %collective-permute-start.5) | collective-permute-done | bytes 262176 | tf_op jit(solution)/shard_map/ppermute | solution.py:117
  152.9 6.2 %collective-permute-done.6 = bf16[32,8,2,256]{3,1,2,0:T(8,128)(2,1)} collective-permute-done((bf16[32,8,2,256]{3,1,2,0:T(8,128)(2,1)S(1)}, bf16[32,8,2,256]{3,1,2,0:T(8,128)(2,1)}, u32[]{:S(2)}, u32[]{:S(2)}) %collective-permute-start.6) | collective-permute-done | bytes 262176 | tf_op jit(solution)/shard_map/ppermute | solution.py:117
  159.2 6.8 %collective-permute-done.7 = bf16[32,8,2,256]{3,1,2,0:T(8,128)(2,1)S(1)} collective-permute-done((bf16[32,8,2,256]{3,1,2,0:T(8,128)(2,1)}, bf16[32,8,2,256]{3,1,2,0:T(8,128)(2,1)S(1)}, u32[]{:S(2)}, u32[]{:S(2)}) %collective-permute-start.7) | collective-permute-done | bytes 262176 | tf_op jit(solution)/shard_map/ppermute | solution.py:117
  167.1 5.7 %collective-permute-done.8 = bf16[32,8,2,256]{3,1,2,0:T(8,128)(2,1)S(1)} collective-permute-done((bf16[32,8,2,256]{3,1,2,0:T(8,128)(2,1)S(1)}, bf16[32,8,2,256]{3,1,2,0:T(8,128)(2,1)S(1)}, u32[]{:S(2)}, u32[]{:S(2)}) %collective-permute-start.8) | collective-permute-done | bytes 262176 | tf_op jit(solution)/shard_map/ppermute | solution.py:117
  173.3 1.4 fusion.48
  174.7 1.4 fusion.49
  176.7 7.6 %convert_bitcast_fusion = bf16[1,1,1024,2048]{3,2,1,0:T(8,128)(2,1)} fusion(bf16[256,1024]{1,0:T(8,128)(2,1)S(1)} %get-tuple-element.6, bf16[256,1024]{1,0:T(8,128)(2,1)S(1)} %get-tuple-element.5, f32[1024]{0:T(1024)S(1)} %multiply_add_fusion.1), kind=kOutput, calls=%fused_computation.8 | convolution fusion | flops 1088421888 | bytes 5246976 | tf_op jit(solution)/shard_map/dot_general | solution.py:86
  (49 shorter events, 7.4 us)
Async XLA Ops:
  2.9 8.4 %collective-permute-start = (bf16[2,256,128]{1,2,0:T(8,128)(2,1)S(1)}, bf16[2,256,128]{1,2,0:T(8,128)(2,1)S(1)}, u32[]{:S(2)}, u32[]{:S(2)}) collective-permute-start(bf16[2,256,128]{1,2,0:T(8,128)(2,1)S(1)} %slice.51), channel_id=1, source_target_pairs={{8,0},{16,8},{24,16},{9,1},{17,9},{25,17},{10,2},{18,10},{26,18},{... | collective-permute-start | bytes 393224 | tf_op jit(solution)/shard_map/ppermute | solution.py:17
  24.6 4.3 %copy-start = (bf16[1,256,16,256]{3,2,1,0:T(8,128)(2,1)S(1)}, bf16[1,256,16,256]{3,2,1,0:T(8,128)(2,1)}, u32[]{:S(2)}) copy-start(bf16[1,256,16,256]{3,2,1,0:T(8,128)(2,1)} %copy.22) | copy-start | bytes 6291460
  24.6 4.3 %copy-start.1 = (f32[4096,128]{1,0:T(8,128)S(1)}, f32[4096,128]{1,0:T(8,128)}, u32[]{:S(2)}) copy-start(f32[4096,128]{1,0:T(8,128)} %fusion.63) | copy-start | bytes 6291460
  34.2 1.2 copy-start.2
  34.7 2.1 %copy-start.3 = (s32[1,32]{1,0:T(1,128)S(1)}, s32[1,32]{1,0:T(1,128)}, u32[]{:S(2)}) copy-start(s32[1,32]{1,0:T(1,128)} %param.5) | copy-start | bytes 388
  35.5 9.4 %collective-permute-start.1 = (bf16[2,256,256]{2,1,0:T(8,128)(2,1)S(1)}, bf16[2,256,256]{2,1,0:T(8,128)(2,1)S(1)}, u32[]{:S(2)}, u32[]{:S(2)}) collective-permute-start(bf16[2,256,256]{2,1,0:T(8,128)(2,1)S(1)} %slice.56), channel_id=1, source_target_pairs={{8,0},{16,8},{24,16},{9,1},{17,9},{25,17},{10,2},{18,10},{26,18},{... | collective-permute-start | bytes 786440 | tf_op jit(solution)/shard_map/ppermute | solution.py:17
  117.3 14.9 %copy-start.4 = (s32[1,1,8]{2,1,0:T(1,128)S(1)}, s32[1,1,8]{2,1,0:T(1,128)}, u32[]{:S(2)}) copy-start(s32[1,1,8]{2,1,0:T(1,128)} %param.4) | copy-start | bytes 100
  125.5 6.7 %collective-permute-start.2 = (bf16[32,8,2,256]{3,1,2,0:T(8,128)(2,1)S(1)}, bf16[32,8,2,256]{3,1,2,0:T(8,128)(2,1)S(1)}, u32[]{:S(2)}, u32[]{:S(2)}) collective-permute-start(bf16[32,8,2,256]{3,1,2,0:T(8,128)(2,1)S(1)} %copy.25), channel_id=1, source_target_pairs={{0,1},{1,2},{2,3},{3,4},{4,5},{5,6},{6,7},{7,0},{8,9},{9,10},{10,1... | collective-permute-start | bytes 786440 | tf_op jit(solution)/shard_map/ppermute | solution.py:117
  132.2 6.7 %collective-permute-start.3 = (bf16[32,8,2,256]{3,1,2,0:T(8,128)(2,1)S(1)}, bf16[32,8,2,256]{3,1,2,0:T(8,128)(2,1)S(1)}, u32[]{:S(2)}, u32[]{:S(2)}) collective-permute-start(bf16[32,8,2,256]{3,1,2,0:T(8,128)(2,1)S(1)} %collective-permute-done.2), channel_id=1, source_target_pairs={{0,1},{1,2},{2,3},{3,4},{4,5},{5,6},{6,7},{7,0},{8,9},{9,10},{10,1... | collective-permute-start | bytes 786440 | tf_op jit(solution)/shard_map/ppermute | solution.py:117
  138.9 6.7 %collective-permute-start.4 = (bf16[32,8,2,256]{3,1,2,0:T(8,128)(2,1)S(1)}, bf16[32,8,2,256]{3,1,2,0:T(8,128)(2,1)S(1)}, u32[]{:S(2)}, u32[]{:S(2)}) collective-permute-start(bf16[32,8,2,256]{3,1,2,0:T(8,128)(2,1)S(1)} %collective-permute-done.3), channel_id=1, source_target_pairs={{0,1},{1,2},{2,3},{3,4},{4,5},{5,6},{6,7},{7,0},{8,9},{9,10},{10,1... | collective-permute-start | bytes 786440 | tf_op jit(solution)/shard_map/ppermute | solution.py:117
  145.6 6.7 %collective-permute-start.5 = (bf16[32,8,2,256]{3,1,2,0:T(8,128)(2,1)S(1)}, bf16[32,8,2,256]{3,1,2,0:T(8,128)(2,1)S(1)}, u32[]{:S(2)}, u32[]{:S(2)}) collective-permute-start(bf16[32,8,2,256]{3,1,2,0:T(8,128)(2,1)S(1)} %collective-permute-done.4), channel_id=1, source_target_pairs={{0,1},{1,2},{2,3},{3,4},{4,5},{5,6},{6,7},{7,0},{8,9},{9,10},{10,1... | collective-permute-start | bytes 786440 | tf_op jit(solution)/shard_map/ppermute | solution.py:117
  152.3 6.8 %collective-permute-start.6 = (bf16[32,8,2,256]{3,1,2,0:T(8,128)(2,1)S(1)}, bf16[32,8,2,256]{3,1,2,0:T(8,128)(2,1)}, u32[]{:S(2)}, u32[]{:S(2)}) collective-permute-start(bf16[32,8,2,256]{3,1,2,0:T(8,128)(2,1)S(1)} %collective-permute-done.5), channel_id=1, source_target_pairs={{0,1},{1,2},{2,3},{3,4},{4,5},{5,6},{6,7},{7,0},{8,9},{9,10},{10,1... | collective-permute-start | bytes 786440 | tf_op jit(solution)/shard_map/ppermute | solution.py:117
  159.1 6.9 %collective-permute-start.7 = (bf16[32,8,2,256]{3,1,2,0:T(8,128)(2,1)}, bf16[32,8,2,256]{3,1,2,0:T(8,128)(2,1)S(1)}, u32[]{:S(2)}, u32[]{:S(2)}) collective-permute-start(bf16[32,8,2,256]{3,1,2,0:T(8,128)(2,1)} %collective-permute-done.6), channel_id=1, source_target_pairs={{0,1},{1,2},{2,3},{3,4},{4,5},{5,6},{6,7},{7,0},{8,9},{9,10},{10,1... | collective-permute-start | bytes 786440 | tf_op jit(solution)/shard_map/ppermute | solution.py:117
  166.0 6.7 %collective-permute-start.8 = (bf16[32,8,2,256]{3,1,2,0:T(8,128)(2,1)S(1)}, bf16[32,8,2,256]{3,1,2,0:T(8,128)(2,1)S(1)}, u32[]{:S(2)}, u32[]{:S(2)}) collective-permute-start(bf16[32,8,2,256]{3,1,2,0:T(8,128)(2,1)S(1)} %collective-permute-done.7), channel_id=1, source_target_pairs={{0,1},{1,2},{2,3},{3,4},{4,5},{5,6},{6,7},{7,0},{8,9},{9,10},{10,1... | collective-permute-start | bytes 786440 | tf_op jit(solution)/shard_map/ppermute | solution.py:117
